TPU v7x, 32 devices: a whole 2x2x4 slice. The times are simulated.
32 devices in a mesh: groups: 2 (over x), gz: 16 (over z, y, core).
Axes of the slice: x: 2, y: 2, z: 4, core: 2. Of those that a mesh axis runs over, the one named last changes fastest.
Arguments:
- labels: int32 [128, 256, 256], P(('groups', 'gz')), parts along dimension 0, may hold values from 0 to 7
- tensor_table: float32 [16, 7], P('groups'), parts along dimension 0, may hold values from -0.3 to 3.5, as said below
- bounds: float32 [4], P('groups'), parts along dimension 0, may hold values from 0 to 51, as said below
- right_side: float32 [128, 256, 256], P(('groups', 'gz')), parts along dimension 0, may hold values from -18 to 18
Outputs:
- solution: float32 [128, 256, 256], P(('groups', 'gz')), parts along dimension 0
- residual: float32 [128, 256, 256], P(('groups', 'gz')), parts along dimension 0
- residual_norm: float32 [2], P('groups'), parts along dimension 0
There are 2 independent parts, one for each index of `groups`. A program takes and returns all parts, laid end to end along the dimension named above; each array names one. Nothing has to cross between parts.
Inputs may be any that keep to these rules, and one draw needn't show every extreme that they name: `tensor_table`: every tensor is diagonally dominant: each diagonal component exceeds the sum of the magnitudes of its row's off-diagonal components by 0.4 or more; reactions are positive. 0 < bounds[0] < bounds[1], and bounds[1] is at least the largest eigenvalue of the operator.
All inputs are finite; a program needn't handle non-finite values.
Results may differ from a plain program's by a relative error of at most 0.00002.
Values sent between devices are 32-bit elements; how exact they have to be, the bound alone decides.
A program may use at most 256 MiB of HBM per device.

v0:
```python
import jax
import jax.numpy as jnp
from jax import lax
from jax.sharding import PartitionSpec as P

ITERS = 3


lattice_steps = (
    (1, 0, 0),
    (0, 1, 0),
    (0, 0, 1),
    (1, 1, 0),
    (1, -1, 0),
    (1, 0, 1),
    (1, 0, -1),
    (0, 1, 1),
    (0, 1, -1),
)
x_links = (0, 3, 4, 5, 6)


def extended_2(cells, sides, width):
    for axis, dim in sides:
        count = lax.axis_size(axis)
        ends = count - 1
        head = lax.slice_in_dim(cells, 0, width, axis=dim)
        tail = lax.slice_in_dim(cells, cells.shape[dim] - width, cells.shape[dim], axis=dim)
        cells = jnp.concatenate(
            [
                lax.ppermute(tail, axis, [(i, (i + 1) % count) for i in range(ends)]),
                cells,
                lax.ppermute(head, axis, [((i + 1) % count, i) for i in range(ends)]),
            ],
            axis=dim,
        )
    return cells


def phase_weights(tensor_table):
    k_xx = tensor_table[:, 0]
    k_yy = tensor_table[:, 1]
    k_zz = tensor_table[:, 2]
    k_xy = tensor_table[:, 3]
    k_xz = tensor_table[:, 4]
    k_yz = tensor_table[:, 5]
    weights = [
        k_xx - jnp.abs(k_xy) - jnp.abs(k_xz),
        k_yy - jnp.abs(k_xy) - jnp.abs(k_yz),
        k_zz - jnp.abs(k_xz) - jnp.abs(k_yz),
        jnp.maximum(k_xy, 0.0),
        jnp.maximum(-k_xy, 0.0),
        jnp.maximum(k_xz, 0.0),
        jnp.maximum(-k_xz, 0.0),
        jnp.maximum(k_yz, 0.0),
        jnp.maximum(-k_yz, 0.0),
    ]
    return (weights, tensor_table[:, 6])


def cell_values(per_phase, labels):
    result = jnp.zeros(labels.shape, jnp.float32)
    for phase in range(per_phase.shape[0]):
        result = jnp.where(labels == phase, per_phase[phase], result)
    return result


def shifted(field, shift_x, shift_y, shift_z):
    length, rows, columns = field.shape
    padded = jnp.pad(field, ((0, 0), (1, 1), (1, 1)))
    return padded[
        1 + shift_x : length - 1 + shift_x,
        1 + shift_y : 1 + shift_y + rows,
        1 + shift_z : 1 + shift_z + columns,
    ]


def apply_operator(field, weights, reaction):
    middle_field = field[1:-1]
    image = reaction[1:-1] * middle_field
    for which, offset in enumerate(lattice_steps):
        own_weight = weights[which][1:-1]
        for direction_sign in (1, -1):
            step_x = direction_sign * offset[0]
            step_y = direction_sign * offset[1]
            step_z = direction_sign * offset[2]
            neighbour = shifted(field, step_x, step_y, step_z)
            link = 0.5 * (own_weight + shifted(weights[which], step_x, step_y, step_z))
            image = image + link * (middle_field - neighbour)
    return image


def pad_planes(field):
    return jnp.pad(field, ((1, 1), (0, 0), (0, 0)))


def per_device(labels, tensor_table, bounds, right_side):
    per_phase, reaction_phase = phase_weights(tensor_table)
    per_cell = [cell_values(table_column, labels) for table_column in per_phase]
    reaction_cell = cell_values(reaction_phase, labels)
    lower_bound = bounds[0]
    upper_bound = bounds[1]
    centre = (upper_bound + lower_bound) / 2.0
    spread = (upper_bound - lower_bound) / 2.0
    sigma_ratio = centre / spread
    factor = 1.0 / sigma_ratio
    solution = jnp.zeros_like(right_side)
    x_weights = jnp.stack([per_cell[which] for which in x_links])
    extended = extended_2(x_weights, (("gz", 1),), 1)
    weights = []
    for which in range(len(lattice_steps)):
        if which in x_links:
            weights.append(extended[x_links.index(which)])
        else:
            weights.append(pad_planes(per_cell[which]))
    reaction = pad_planes(reaction_cell)
    residual = right_side
    direction = right_side / centre
    for iteration in range(ITERS):
        solution = solution + direction
        direction_rim = extended_2(direction, (("gz", 0),), 1)
        image = apply_operator(direction_rim, weights, reaction)
        residual = residual - image
        new_factor = 1.0 / (2.0 * sigma_ratio - factor)
        direction = new_factor * factor * direction + 2.0 * new_factor / spread * residual
        factor = new_factor
    squares = lax.psum(jnp.sum(residual * residual), "gz")
    residual_norm = jnp.sqrt(squares).reshape(1)
    return (solution, residual, residual_norm)


def solution(mesh):
    return jax.shard_map(
        per_device,
        mesh=mesh,
        in_specs=(
            P(("groups", "gz"), None, None),
            P("groups", None),
            P("groups"),
            P(("groups", "gz"), None, None),
        ),
        out_specs=(P(("groups", "gz"), None, None), P(("groups", "gz"), None, None), P("groups")),
        check_vma=False,
    )
```

profile of v0, /device:TPU:0, one launch (start us, length us, event | category | flops | bytes accessed | tf_op | source)
XLA Modules:
  0.0 196.1 jit_solution(2028619274310046077)
XLA Ops:
  5.6 2.4 %collective-permute-start.3 = (f32[1,256,256]{2,1,0:T(8,128)}, f32[1,256,256]{2,1,0:T(8,128)S(1)}, u32[]{:S(2)}, u32[]{:S(2)}) collective-permute-start(f32[1,256,256]{2,1,0:T(8,128)} %get-tuple-element.41), channel_id=1, source_target_pairs={{0,1},{1,2},{2,3},{3,4},{4,5},{5,6},{6,7},{7,8},{8,9},{9,10},{10,1... | collective-permute-start | bytes 786440 | tf_op jit(solution)/shard_map/ppermute | solution.py:31
  12.0 6.4 %select_select_fusion.3 = (f32[4,256,256]{2,1,0:T(8,128)S(1)}, pred[4,256,256]{2,1,0:T(8,128)(4,1)S(1)}, pred[4,256,256]{2,1,0:T(8,128)(4,1)S(1)}, pred[4,256,25...) fusion(f32[]{:T(128)} %bitcast.64, f32[]{:T(128)} %bitcast.63, ...), kind=kLoop, calls=%fused_computation.258 | loop fusion | flops 4194304 | bytes 4194336 | tf_op jit(solution)/shard_map/jit(_where)/select_n | solution.py:64
  18.4 6.7 %bitcast_dynamic-update-slice_fusion.4 = (f32[5,4,256,256]{3,2,1,0:T(8,128)S(1)}, f32[4,256,256]{2,1,0:T(8,128)}) fusion(pred[4,256,256]{2,1,0:T(8,128)(4,1)S(1)} %get-tuple-element.20, pred[4,256,256]{2,1,0:T(8,128)(4,1)S(1)} %get-tuple-element.19, pred[4,256,256]{2,1,0:T(8,128)(4,1)S(1)} %get-tuple-element.18, ...), kind=kLoop, calls=%fused_computation.250 | loop fusion | flops 2097151 | bytes 4194336
  25.1 6.8 %bitcast_dynamic-update-slice_fusion.3 = (f32[5,4,256,256]{3,2,1,0:T(8,128)S(1)}, f32[4,256,256]{2,1,0:T(8,128)}) fusion(f32[5,4,256,256]{3,2,1,0:T(8,128)S(1)} %get-tuple-element.29, pred[4,256,256]{2,1,0:T(8,128)(4,1)S(1)} %get-tuple-element.20, pred[4,256,256]{2,1,0:T(8,128)(4,1)S(1)} %get-tuple-element.19, ...), kind=kLoop, calls=%fused_computation.249 | loop fusion | flops 2097152 | bytes 4194336
  31.9 6.8 %bitcast_dynamic-update-slice_fusion.2 = (f32[5,4,256,256]{3,2,1,0:T(8,128)S(1)}, f32[4,256,256]{2,1,0:T(8,128)}) fusion(f32[5,4,256,256]{3,2,1,0:T(8,128)S(1)} %get-tuple-element.27, pred[4,256,256]{2,1,0:T(8,128)(4,1)S(1)} %get-tuple-element.20, pred[4,256,256]{2,1,0:T(8,128)(4,1)S(1)} %get-tuple-element.19, ...), kind=kLoop, calls=%fused_computation.248 | loop fusion | flops 2097152 | bytes 4194336
  38.7 6.8 %bitcast_dynamic-update-slice_fusion.1 = (f32[5,4,256,256]{3,2,1,0:T(8,128)S(1)}, f32[4,256,256]{2,1,0:T(8,128)}) fusion(f32[5,4,256,256]{3,2,1,0:T(8,128)S(1)} %get-tuple-element.25, pred[4,256,256]{2,1,0:T(8,128)(4,1)S(1)} %get-tuple-element.20, pred[4,256,256]{2,1,0:T(8,128)(4,1)S(1)} %get-tuple-element.19, ...), kind=kLoop, calls=%fused_computation.247 | loop fusion | flops 2097152 | bytes 4194336
  45.5 6.8 %bitcast_dynamic-update-slice_fusion = (f32[5,4,256,256]{3,2,1,0:T(8,128)S(1)}, f32[4,256,256]{2,1,0:T(8,128)}) fusion(f32[5,4,256,256]{3,2,1,0:T(8,128)S(1)} %get-tuple-element.23, pred[4,256,256]{2,1,0:T(8,128)(4,1)S(1)} %get-tuple-element.20, pred[4,256,256]{2,1,0:T(8,128)(4,1)S(1)} %get-tuple-element.19, pred[4,256,256]{2,1,0:T(8,128)(4,1)S(1)} %get-tuple-element.18, ...), kind=kLoop, calls=%fused_computation.246 | loop fusion | flops 2097152 | bytes 4194336 | tf_op jit(solution)/shard_map/stack | solution.py:108
  52.3 1.9 fusion.165
  55.4 6.3 %collective-permute-start.2 = (f32[5,1,256,256]{3,2,1,0:T(8,128)}, f32[5,1,256,256]{3,2,1,0:T(8,128)}, u32[]{:S(2)}, u32[]{:S(2)}) collective-permute-start(f32[5,1,256,256]{3,2,1,0:T(8,128)} %get-tuple-element.35), channel_id=1, source_target_pairs={{0,1},{1,2},{2,3},{3,4},{4,5},{5,6},{6,7},{7,8},{8,9},{9,10},{10,1... | collective-permute-start | bytes 3932168 | tf_op jit(solution)/shard_map/ppermute | solution.py:31
  63.8 6.8 %select_select_fusion.1 = f32[4,256,256]{2,1,0:T(8,128)} fusion(pred[4,256,256]{2,1,0:T(8,128)(4,1)S(1)} %get-tuple-element.20, pred[4,256,256]{2,1,0:T(8,128)(4,1)S(1)} %get-tuple-element.19, pred[4,256,256]{2,1,0:T(8,128)(4,1)S(1)} %get-tuple-element.18, pred[4,256,256]{2,1,0:T(8,128)(4,1)S(1)} %get-tuple-element.17, ...), kind=kLoop, calls=%fused_computation.256 | loop fusion | flops 2097152 | bytes 3145760 | tf_op jit(solution)/shard_map/jit(_where)/select_n | solution.py:64
  72.8 7.0 %select_select_fusion.2 = f32[4,256,256]{2,1,0:T(8,128)} fusion(pred[4,256,256]{2,1,0:T(8,128)(4,1)S(1)} %get-tuple-element.20, pred[4,256,256]{2,1,0:T(8,128)(4,1)S(1)} %get-tuple-element.19, pred[4,256,256]{2,1,0:T(8,128)(4,1)S(1)} %get-tuple-element.18, pred[4,256,256]{2,1,0:T(8,128)(4,1)S(1)} %get-tuple-element.17, ...), kind=kLoop, calls=%fused_computation.257 | loop fusion | flops 2097152 | bytes 3145760 | tf_op jit(solution)/shard_map/jit(_where)/select_n | solution.py:64
  79.8 7.0 %select_select_fusion = f32[4,256,256]{2,1,0:T(8,128)} fusion(pred[4,256,256]{2,1,0:T(8,128)(4,1)S(1)} %get-tuple-element.20, pred[4,256,256]{2,1,0:T(8,128)(4,1)S(1)} %get-tuple-element.19, pred[4,256,256]{2,1,0:T(8,128)(4,1)S(1)} %get-tuple-element.18, pred[4,256,256]{2,1,0:T(8,128)(4,1)S(1)} %get-tuple-element.17, ...), kind=kLoop, calls=%fused_computation.255 | loop fusion | flops 2097152 | bytes 3145760 | tf_op jit(solution)/shard_map/jit(_where)/select_n | solution.py:64
  86.8 1.7 select_maximum_fusion.4
  88.5 2.1 %maximum_bitcast_fusion.2 = (f32[6,256,256]{2,1,0:T(8,128)S(1)}, f32[6,256,256]{2,1,0:T(8,128)S(1)}, f32[6,256,256]{2,1,0:T(8,128)S(1)}, f32[6,256,256]{2,1,0:T(8,128)S(1)}) fusion(f32[5,1,256,256]{3,2,1,0:T(8,128)} %collective-permute-done, f32[5,4,256,256]{3,2,1,0:T(8,128)S(1)} %copy-done.1, f32[5,1,256,256]{3,2,1,0:T(8,128)} %collective-permute-done.2), kind=kLoop, calls=%fused_computation.34 | loop fusion | flops 3145728 | bytes 14155776 | tf_op jit(solution)/shard_map/squeeze | solution.py:113
  90.7 18.2 %multiply_add_fusion.1 = (f32[4,256,256]{2,1,0:T(8,128)}, f32[4,256,256]{2,1,0:T(8,128)}, f32[4,256,256]{2,1,0:T(8,128)}, f32[4,256,256]{2,1,0:T(8,128)}, f32[4,256,256]{2,1,0:T(8,128)}) fusion(f32[4,256,256]{2,1,0:T(8,128)} %copy-done.20, f32[]{:T(128)S(6)} %div.43, f32[]{:T(128)S(6)} %mul.305, f32[4,256,256]{2,1,0:T(8,128)} %param.7, ...), kind=kLoop, calls=%fused_computation.254 | loop fusion | flops 28049408 | bytes 50331688 | tf_op jit(solution)/shard_map/add | solution.py:125
  108.9 2.0 %fusion.167 = (f32[1,256,256]{2,1,0:T(8,128)}, f32[1,256,256]{2,1,0:T(8,128)}) fusion(f32[4,256,256]{2,1,0:T(8,128)} %get-tuple-element.7), kind=kLoop, calls=%fused_computation.285 | loop fusion | bytes 1048576 | tf_op jit(solution)/shard_map/slice | solution.py:28
  110.9 4.6 %collective-permute-start.5 = (f32[1,256,256]{2,1,0:T(8,128)}, f32[1,256,256]{2,1,0:T(8,128)S(1)}, u32[]{:S(2)}, u32[]{:S(2)}) collective-permute-start(f32[1,256,256]{2,1,0:T(8,128)} %get-tuple-element.39), channel_id=1, source_target_pairs={{0,1},{1,2},{2,3},{3,4},{4,5},{5,6},{6,7},{7,8},{8,9},{9,10},{10,1... | collective-permute-start | bytes 786440 | tf_op jit(solution)/shard_map/ppermute | solution.py:31
  116.9 4.3 %collective-permute-done.4 = f32[1,256,256]{2,1,0:T(8,128)} collective-permute-done((f32[1,256,256]{2,1,0:T(8,128)}, f32[1,256,256]{2,1,0:T(8,128)}, u32[]{:S(2)}, u32[]{:S(2)}) %collective-permute-start.4) | collective-permute-done | bytes 262176 | tf_op jit(solution)/shard_map/ppermute | solution.py:33
  121.2 2.1 %select_maximum_fusion.2 = f32[6,258,258]{2,1,0:T(8,128)S(1)} fusion(f32[1,256,256]{2,1,0:T(8,128)} %collective-permute-done.4, f32[4,256,256]{2,1,0:T(8,128)} %get-tuple-element.7, f32[1,256,256]{2,1,0:T(8,128)S(1)} %collective-permute-done.5), kind=kLoop, calls=%fused_computation.22 | loop fusion | flops 5990760 | bytes 3170400 | tf_op jit(solution)/shard_map/concatenate | solution.py:29
  123.4 14.1 %multiply_add_fusion = (f32[4,256,256]{2,1,0:T(8,128)S(1)}, f32[4,256,256]{2,1,0:T(8,128)S(1)}) fusion(f32[4,256,256]{2,1,0:T(8,128)} %get-tuple-element.7, f32[]{:T(128)S(6)} %div.45, f32[]{:T(128)S(6)} %mul.348, f32[4,256,256]{2,1,0:T(8,128)} %get-tuple-element.8, f32[6,258,258]{2,1,0:T(8,128)S(1)} %select_maximum_fusion.2, ...), kind=kLoop, calls=%fused_computation.252 | loop fusion | flops 24379392 | bytes 39321608 | tf_op jit(solution)/shard_map/add | solution.py:125
  137.6 6.8 %collective-permute-start.7 = (f32[1,256,256]{2,1,0:T(8,128)S(1)}, f32[1,256,256]{2,1,0:T(8,128)S(1)}, u32[]{:S(2)}, u32[]{:S(2)}) collective-permute-start(f32[1,256,256]{2,1,0:T(8,128)S(1)} %get-tuple-element.37), channel_id=1, source_target_pairs={{0,1},{1,2},{2,3},{3,4},{4,5},{5,6},{6,7},{7,8},{8,9},{9,10},{10,1... | collective-permute-start | bytes 786440 | tf_op jit(solution)/shard_map/ppermute | solution.py:31
  144.4 1.5 collective-permute-start.6
  149.9 10.1 %multiply_reduce_fusion = (f32[]{:T(128)}, f32[4,256,256]{2,1,0:T(8,128)}) fusion(f32[4,256,256]{2,1,0:T(8,128)S(1)} %get-tuple-element.6, f32[4,256,256]{2,1,0:T(8,128)S(1)} %get-tuple-element.5, f32[6,258,258]{2,1,0:T(8,128)S(1)} %select_maximum_fusion, f32[4,256,256]{2,1,0:T(8,128)S(1)} %copy-done.19, f32[4,256,256]{2,1,0:T(8,128)S(1)} %copy-done.17, ...), kind=kLoop, calls=%fused_computation.251 | loop fusion | flops 24117248 | bytes 38273028 | tf_op jit(solution)/shard_map/reduce_sum | solution.py:127
  160.0 34.3 %psum.7 = f32[]{:T(128)} all-reduce(f32[]{:T(128)} %get-tuple-element.3), channel_id=1, replica_groups=mesh['groups'=2,'gz'=16] {'gz'}, use_global_device_ids=true, to_apply=%region_1.2 | all-reduce | flops 1 | bytes 8 | tf_op jit(solution)/shard_map/psum | solution.py:127
  (85 shorter events, 16.8 us)
Async XLA Ops:
  0.6 11.4 %copy-start.29 = (s32[4,256,256]{2,1,0:T(8,128)S(1)}, s32[4,256,256]{2,1,0:T(8,128)}, u32[]{:S(2)}) copy-start(s32[4,256,256]{2,1,0:T(8,128)} %param.4) | copy-start | bytes 3145732
  5.6 81.1 %collective-permute-start.3 = (f32[1,256,256]{2,1,0:T(8,128)}, f32[1,256,256]{2,1,0:T(8,128)S(1)}, u32[]{:S(2)}, u32[]{:S(2)}) collective-permute-start(f32[1,256,256]{2,1,0:T(8,128)} %get-tuple-element.41), channel_id=1, source_target_pairs={{0,1},{1,2},{2,3},{3,4},{4,5},{5,6},{6,7},{7,8},{8,9},{9,10},{10,1... | collective-permute-start | bytes 786440 | tf_op jit(solution)/shard_map/ppermute | solution.py:31
  8.0 78.7 %collective-permute-start.1 = (f32[1,256,256]{2,1,0:T(8,128)}, f32[1,256,256]{2,1,0:T(8,128)}, u32[]{:S(2)}, u32[]{:S(2)}) collective-permute-start(f32[1,256,256]{2,1,0:T(8,128)} %get-tuple-element.42), channel_id=1, source_target_pairs={{1,0},{2,1},{3,2},{4,3},{5,4},{6,5},{7,6},{8,7},{9,8},{10,9},{11,1... | collective-permute-start | bytes 786440 | tf_op jit(solution)/shard_map/ppermute | solution.py:33
  18.4 72.2 %copy-start.11 = (f32[4,256,256]{2,1,0:T(8,128)}, f32[4,256,256]{2,1,0:T(8,128)S(1)}, u32[]{:S(2)}) copy-start(f32[4,256,256]{2,1,0:T(8,128)S(1)} %get-tuple-element.12) | copy-start | bytes 3145732
  55.4 33.1 %collective-permute-start.2 = (f32[5,1,256,256]{3,2,1,0:T(8,128)}, f32[5,1,256,256]{3,2,1,0:T(8,128)}, u32[]{:S(2)}, u32[]{:S(2)}) collective-permute-start(f32[5,1,256,256]{3,2,1,0:T(8,128)} %get-tuple-element.35), channel_id=1, source_target_pairs={{0,1},{1,2},{2,3},{3,4},{4,5},{5,6},{6,7},{7,8},{8,9},{9,10},{10,1... | collective-permute-start | bytes 3932168 | tf_op jit(solution)/shard_map/ppermute | solution.py:31
  61.7 26.8 %collective-permute-start = (f32[5,1,256,256]{3,2,1,0:T(8,128)}, f32[5,1,256,256]{3,2,1,0:T(8,128)}, u32[]{:S(2)}, u32[]{:S(2)}) collective-permute-start(f32[5,1,256,256]{3,2,1,0:T(8,128)} %get-tuple-element.36), channel_id=1, source_target_pairs={{1,0},{2,1},{3,2},{4,3},{5,4},{6,5},{7,6},{8,7},{9,8},{10,9},{11,1... | collective-permute-start | bytes 3932168 | tf_op jit(solution)/shard_map/ppermute | solution.py:33
  72.8 14.0 %copy-start.21 = (f32[4,256,256]{2,1,0:T(8,128)S(1)}, f32[4,256,256]{2,1,0:T(8,128)}, u32[]{:S(2)}) copy-start(f32[4,256,256]{2,1,0:T(8,128)} %copy-done.20) | copy-start | bytes 3145732
  90.6 18.3 %copy-start.2 = (f32[6,256,256]{2,1,0:T(8,128)}, f32[6,256,256]{2,1,0:T(8,128)S(1)}, u32[]{:S(2)}) copy-start(f32[6,256,256]{2,1,0:T(8,128)S(1)} %get-tuple-element.31) | copy-start | bytes 4718596
  90.6 18.3 %copy-start.4 = (f32[6,256,256]{2,1,0:T(8,128)}, f32[6,256,256]{2,1,0:T(8,128)S(1)}, u32[]{:S(2)}) copy-start(f32[6,256,256]{2,1,0:T(8,128)S(1)} %get-tuple-element.32) | copy-start | bytes 4718596
  90.7 18.3 %copy-start.6 = (f32[6,256,256]{2,1,0:T(8,128)}, f32[6,256,256]{2,1,0:T(8,128)S(1)}, u32[]{:S(2)}) copy-start(f32[6,256,256]{2,1,0:T(8,128)S(1)} %get-tuple-element.33) | copy-start | bytes 4718596
  90.7 18.3 %copy-start.8 = (f32[6,256,256]{2,1,0:T(8,128)}, f32[6,256,256]{2,1,0:T(8,128)S(1)}, u32[]{:S(2)}) copy-start(f32[6,256,256]{2,1,0:T(8,128)S(1)} %get-tuple-element.34) | copy-start | bytes 4718596
  108.9 14.4 %copy-start.3 = (f32[6,256,256]{2,1,0:T(8,128)S(1)}, f32[6,256,256]{2,1,0:T(8,128)}, u32[]{:S(2)}) copy-start(f32[6,256,256]{2,1,0:T(8,128)} %copy-done.2) | copy-start | bytes 4718596
  108.9 14.4 %copy-start.5 = (f32[6,256,256]{2,1,0:T(8,128)S(1)}, f32[6,256,256]{2,1,0:T(8,128)}, u32[]{:S(2)}) copy-start(f32[6,256,256]{2,1,0:T(8,128)} %copy-done.4) | copy-start | bytes 4718596
  110.9 6.0 %collective-permute-start.5 = (f32[1,256,256]{2,1,0:T(8,128)}, f32[1,256,256]{2,1,0:T(8,128)S(1)}, u32[]{:S(2)}, u32[]{:S(2)}) collective-permute-start(f32[1,256,256]{2,1,0:T(8,128)} %get-tuple-element.39), channel_id=1, source_target_pairs={{0,1},{1,2},{2,3},{3,4},{4,5},{5,6},{6,7},{7,8},{8,9},{9,10},{10,1... | collective-permute-start | bytes 786440 | tf_op jit(solution)/shard_map/ppermute | solution.py:31
  115.5 5.7 %collective-permute-start.4 = (f32[1,256,256]{2,1,0:T(8,128)}, f32[1,256,256]{2,1,0:T(8,128)}, u32[]{:S(2)}, u32[]{:S(2)}) collective-permute-start(f32[1,256,256]{2,1,0:T(8,128)} %get-tuple-element.40), channel_id=1, source_target_pairs={{1,0},{2,1},{3,2},{4,3},{5,4},{6,5},{7,6},{8,7},{9,8},{10,9},{11,1... | collective-permute-start | bytes 786440 | tf_op jit(solution)/shard_map/ppermute | solution.py:33
  123.3 22.6 %copy-start.10 = (f32[4,256,256]{2,1,0:T(8,128)S(1)}, f32[4,256,256]{2,1,0:T(8,128)}, u32[]{:S(2)}) copy-start(f32[4,256,256]{2,1,0:T(8,128)} %get-tuple-element.7) | copy-start | bytes 3145732
  123.4 22.6 %copy-start.22 = (f32[4,256,256]{2,1,0:T(8,128)S(1)}, f32[4,256,256]{2,1,0:T(8,128)}, u32[]{:S(2)}) copy-start(f32[4,256,256]{2,1,0:T(8,128)} %param.7) | copy-start | bytes 3145732
  123.4 26.0 %copy-start.19 = (f32[4,256,256]{2,1,0:T(8,128)S(1)}, f32[4,256,256]{2,1,0:T(8,128)}, u32[]{:S(2)}) copy-start(f32[4,256,256]{2,1,0:T(8,128)} %select_select_fusion) | copy-start | bytes 3145732
  123.4 26.0 %copy-start.23 = (f32[4,256,256]{2,1,0:T(8,128)S(1)}, f32[4,256,256]{2,1,0:T(8,128)}, u32[]{:S(2)}) copy-start(f32[4,256,256]{2,1,0:T(8,128)} %get-tuple-element.9) | copy-start | bytes 3145732
  123.4 26.0 %copy-start.24 = (f32[4,256,256]{2,1,0:T(8,128)S(1)}, f32[4,256,256]{2,1,0:T(8,128)}, u32[]{:S(2)}) copy-start(f32[4,256,256]{2,1,0:T(8,128)} %get-tuple-element.10) | copy-start | bytes 3145732
  123.4 26.0 %copy-start.25 = (f32[4,256,256]{2,1,0:T(8,128)S(1)}, f32[4,256,256]{2,1,0:T(8,128)}, u32[]{:S(2)}) copy-start(f32[4,256,256]{2,1,0:T(8,128)} %get-tuple-element.11) | copy-start | bytes 3145732
  137.6 11.9 %copy-start.18 = (f32[4,256,256]{2,1,0:T(8,128)S(1)}, f32[4,256,256]{2,1,0:T(8,128)}, u32[]{:S(2)}) copy-start(f32[4,256,256]{2,1,0:T(8,128)} %select_select_fusion.2) | copy-start | bytes 3145732
  137.6 9.7 %collective-permute-start.7 = (f32[1,256,256]{2,1,0:T(8,128)S(1)}, f32[1,256,256]{2,1,0:T(8,128)S(1)}, u32[]{:S(2)}, u32[]{:S(2)}) collective-permute-start(f32[1,256,256]{2,1,0:T(8,128)S(1)} %get-tuple-element.37), channel_id=1, source_target_pairs={{0,1},{1,2},{2,3},{3,4},{4,5},{5,6},{6,7},{7,8},{8,9},{9,10},{10,1... | collective-permute-start | bytes 786440 | tf_op jit(solution)/shard_map/ppermute | solution.py:31
  144.4 3.4 %collective-permute-start.6 = (f32[1,256,256]{2,1,0:T(8,128)S(1)}, f32[1,256,256]{2,1,0:T(8,128)S(1)}, u32[]{:S(2)}, u32[]{:S(2)}) collective-permute-start(f32[1,256,256]{2,1,0:T(8,128)S(1)} %get-tuple-element.38), channel_id=1, source_target_pairs={{1,0},{2,1},{3,2},{4,3},{5,4},{6,5},{7,6},{8,7},{9,8},{10,9},{11,1... | collective-permute-start | bytes 786440 | tf_op jit(solution)/shard_map/ppermute | solution.py:33
  (15 other events, 63.3 us)
where the time goes:
time: 197 us; the launch traced here: 196 us
  other arithmetic  113 us (57%)
  blocking collectives  34.3 us (17%)
  starting transfers between devices  25.6 us (13%)
  local copies, waits for them, and re-layouts  12.7 us (6%)
  between operations  5.93 us (3%)
  waiting for transfers between devices  4.89 us (2%)
    psum x1, blocking collectives, per_device(): squares = lax.psum(jnp.sum(residual * residual), 'gz')  34.3 us
    add x2, other arithmetic, per_device(): new_factor * factor * direction + 2.0 * new_factor / spread * residual  32.3 us
    select_n x4, other arithmetic, cell_values(): result = jnp.where(labels == phase, per_phase[phase], result)  27.2 us
    unnamed x4, other arithmetic  27 us
    ppermute x4, starting transfers between devices, extended_2(): lax.ppermute(tail, axis, [(i, (i + 1) % count) for i in range(ends)])  20 us
    reduce_sum x1, other arithmetic, per_device(): squares = lax.psum(jnp.sum(residual * residual), 'gz')  10.1 us
    another operation x1, other arithmetic, per_device(): x_weights = jnp.stack([per_cell[which] for which in x_links])  6.79 us
    ppermute x4, starting transfers between devices, extended_2(): lax.ppermute(head, axis, [((i + 1) % count, i) for i in range(ends)])  5.56 us
  transfers between devices with their start and end apart: 8, of which 2 were waited for; matrix products, arithmetic and copies ran while one was open for 36% of the time, Pallas kernels for 0%

commit v1 on v0

v1 whole, which is shorter than its diff:
```python
import functools

import jax
import jax.numpy as jnp
from jax import lax
from jax.experimental import pallas as pl
from jax.experimental.pallas import tpu as pltpu
from jax.sharding import PartitionSpec as P

ITERS = 3
PAD = 8
ROWS = 16
LANES = 128
MESH = pl.DeviceIdType.MESH


def shift_z(t, step):
    count = t.shape[1] // LANES
    lane = lax.broadcasted_iota(jnp.int32, (t.shape[0], LANES), 1)
    parts = [t[:, k * LANES : (k + 1) * LANES] for k in range(count)]
    rolled = [pltpu.roll(part, (LANES - step) % LANES, 1) for part in parts]
    zero = jnp.zeros_like(rolled[0])
    edge = lane == (LANES - 1 if step > 0 else 0)
    result = []
    for k in range(count):
        other = rolled[k + step] if 0 <= k + step < count else zero
        result.append(jnp.where(edge, other, rolled[k]))
    return jnp.concatenate(result, axis=1)


def pos(t):
    return jnp.maximum(t, 0.0)


def neg(t):
    return jnp.maximum(-t, 0.0)


def kernel(
    n, planes, rows, table_ref, bounds_ref, labels_hbm, rhs_hbm,
    solution_hbm, residual_hbm, norm_ref,
    lab, v1, v2, v3, hx, kxy, kxz, hy, hz, kyz, react, coef, diag, res, out_s, out_r,
    weight, partial, gathered, local_sem, out_sem, send_sem, recv_sem, psend, precv,
):
    me = lax.axis_index("gz")
    left, right = me - 1, me + 1
    has_left, has_right = me > 0, me < n - 1
    fields = (v1, v2, v3)
    chunks = rows // ROWS
    body_rows = pl.ds(PAD, rows)

    barrier = pltpu.get_barrier_semaphore()

    def greet(k, carry):
        pl.semaphore_signal(
            barrier, inc=1, device_id={"gz": lax.rem(me + k, n)}, device_id_type=MESH
        )
        return carry

    lax.fori_loop(1, n, greet, 0)

    load_rhs = pltpu.make_async_copy(
        rhs_hbm, v1.at[pl.ds(1, planes), body_rows], local_sem.at[0]
    )
    load_lab = pltpu.make_async_copy(labels_hbm, lab.at[pl.ds(1, planes)], local_sem.at[1])
    load_lab.start()
    load_rhs.start()
    pl.semaphore_wait(barrier, n - 1)

    def views(kind, plane):
        if kind == 0:
            return lab.at[plane]
        return fields[kind - 1].at[plane, body_rows]

    def source(kind, plane):
        if kind == 0:
            return labels_hbm.at[plane]
        if kind == 1:
            return rhs_hbm.at[plane]
        return fields[kind - 1].at[plane + 1, body_rows]

    def to_left(kind):
        return pltpu.make_async_remote_copy(
            src_ref=source(kind, 0),
            dst_ref=views(kind, planes + 1),
            send_sem=send_sem.at[kind, 0],
            recv_sem=recv_sem.at[kind, 0],
            device_id={"gz": left},
            device_id_type=MESH,
        )

    def to_right(kind):
        return pltpu.make_async_remote_copy(
            src_ref=source(kind, planes - 1),
            dst_ref=views(kind, 0),
            send_sem=send_sem.at[kind, 1],
            recv_sem=recv_sem.at[kind, 1],
            device_id={"gz": right},
            device_id_type=MESH,
        )

    def send(kind):
        @pl.when(has_left)
        def _():
            to_left(kind).start()

        @pl.when(has_right)
        def _():
            to_right(kind).start()

    def receive(kind):
        @pl.when(has_left)
        def _():
            to_right(kind).wait_recv()

        @pl.when(has_right)
        def _():
            to_left(kind).wait_recv()

    send(0)
    send(1)

    for phase in range(weight.shape[0]):
        k_xx, k_yy, k_zz, k_xy, k_xz, k_yz, m = [table_ref[phase, c] for c in range(7)]
        weight[phase, 0] = 0.5 * (k_xx - jnp.abs(k_xy) - jnp.abs(k_xz))
        weight[phase, 1] = 0.5 * (k_yy - jnp.abs(k_xy) - jnp.abs(k_yz))
        weight[phase, 2] = 0.5 * (k_zz - jnp.abs(k_xz) - jnp.abs(k_yz))
        weight[phase, 3] = 0.5 * k_xy
        weight[phase, 4] = 0.5 * k_xz
        weight[phase, 5] = 0.5 * k_yz
        weight[phase, 6] = m

    columns = v1.shape[2]
    strip = jnp.zeros((PAD, columns), jnp.float32)
    for ref in (v1, v2, v3, kxy, hy, kyz):
        for plane in range(ref.shape[0]):
            ref[plane, pl.ds(0, PAD)] = strip
            ref[plane, pl.ds(PAD + rows, PAD)] = strip

    def clear(plane):
        zero = jnp.zeros((ROWS, columns), jnp.float32)

        def step(k, carry):
            at = pl.multiple_of(k * ROWS, ROWS)
            for ref in (v1, v2, v3, kxy):
                ref[plane, pl.ds(at + PAD, ROWS)] = zero
            for ref in (hx, kxz):
                ref[plane, pl.ds(at, ROWS)] = zero
            return carry

        lax.fori_loop(0, chunks, step, 0)

    @pl.when(me == 0)
    def _():
        clear(0)

    @pl.when(me == n - 1)
    def _():
        clear(planes + 1)

    def look_up(plane, at, which):
        label = lab[plane, pl.ds(at, ROWS)]
        bits = [(label & b) != 0 for b in (1, 2, 4)]
        out = []
        for column in which:
            level = [
                jnp.full(label.shape, weight[phase, column], jnp.float32)
                for phase in range(8)
            ]
            for bit in bits:
                level = [
                    jnp.where(bit, level[2 * k + 1], level[2 * k])
                    for k in range(len(level) // 2)
                ]
            out.append(level[0])
        return out

    def look_up_x(plane, at):
        hx[plane, pl.ds(at, ROWS)], kxy[plane, pl.ds(at + PAD, ROWS)], kxz[
            plane, pl.ds(at, ROWS)
        ] = look_up(plane, at, (0, 3, 4))

    def own_step(k, carry):
        at = pl.multiple_of(k * ROWS, ROWS)
        for plane in range(planes):
            values = look_up(plane + 1, at, range(7))
            hx[plane + 1, pl.ds(at, ROWS)] = values[0]
            hy[plane, pl.ds(at + PAD, ROWS)] = values[1]
            hz[plane, pl.ds(at, ROWS)] = values[2]
            kxy[plane + 1, pl.ds(at + PAD, ROWS)] = values[3]
            kxz[plane + 1, pl.ds(at, ROWS)] = values[4]
            kyz[plane, pl.ds(at + PAD, ROWS)] = values[5]
            react[plane, pl.ds(at, ROWS)] = values[6]
        return carry

    def three(ref, plane, at):
        wide = ref[plane, pl.ds(at, ROWS + 2 * PAD)]
        total = ROWS + 2 * PAD
        return (
            wide[PAD : PAD + ROWS],
            pltpu.roll(wide, total - 1, 0)[PAD : PAD + ROWS],
            pltpu.roll(wide, 1, 0)[PAD : PAD + ROWS],
        )

    def coefficients(which):
        def step(k, carry):
            at = pl.multiple_of(k * ROWS, ROWS)
            here = pl.ds(at, ROWS)
            for x in which:
                hx0 = hx[x + 1, here]
                hy0, hyp, hym = three(hy, x, at)
                hz0 = hz[x, here]
                k0 = kxy[x + 1, pl.ds(at + PAD, ROWS)]
                _, kpp, kpm = three(kxy, x + 2, at)
                _, kmp, kmm = three(kxy, x, at)
                xz0, xzp, xzm = kxz[x + 1, here], kxz[x + 2, here], kxz[x, here]
                yz0, yzp, yzm = three(kyz, x, at)
                c = [
                    hx0 + hx[x + 2, here],
                    hx0 + hx[x, here],
                    hy0 + hyp,
                    hy0 + hym,
                    pos(k0) + pos(kpp),
                    pos(k0) + pos(kmm),
                    neg(k0) + neg(kpm),
                    neg(k0) + neg(kmp),
                ]
                total = react[x, here] + 2.0 * (hz0 + jnp.abs(xz0) + jnp.abs(yz0))
                for value in c:
                    total = total + value
                for sign, f, g in ((1, pos, neg), (-1, neg, pos)):
                    ends = [hz0, f(xzp), g(xzm), f(yzp), g(yzm)]
                    hz_s, xz_s, yz_s = [shift_z(t, -sign) for t in (hz0, xz0, yz0)]
                    starts = [hz_s, f(xz_s), g(xz_s), f(yz_s), g(yz_s)]
                    c += [a + b for a, b in zip(starts, ends)]
                    total = total + shift_z(sum(ends[1:], ends[0]), sign)
                for index, value in enumerate(c):
                    coef[index, x, here] = value
                diag[x, here] = total
            return carry

        lax.fori_loop(0, chunks, step, 0)

    def image(loaded, at, x):
        here = pl.ds(at, ROWS)
        u, up, um = loaded(x + 2)
        v, vp, vm = loaded(x + 1)
        w, wp, wm = loaded(x)
        flat = (u, w, vp, vm, up, wm, um, wp)
        side = (v, u, w, vp, vm)
        parts = [
            functools.reduce(
                lambda a, b: a + b,
                [coef[first + i, x, here] * t for i, t in enumerate(terms)],
            )
            for first, terms in ((0, flat), (8, side), (13, side))
        ]
        return (
            diag[x, here] * v - parts[0] - shift_z(parts[1], 1) - shift_z(parts[2], -1)
        ), v

    lower, upper = bounds_ref[0], bounds_ref[1]
    shape = (ROWS, columns)
    centre = jnp.full(shape, (upper + lower) / 2.0)
    spread = jnp.full(shape, (upper - lower) / 2.0)
    inverse = 1.0 / centre
    sigma = centre / spread
    factor = 1.0 / sigma
    factors = []
    for _ in range(ITERS - 1):
        new_factor = 1.0 / (2.0 * sigma - factor)
        factors.append((new_factor * factor, 2.0 * new_factor / spread))
        factor = new_factor

    def iterate(iteration, which, total):
        field = fields[iteration]

        def step(k, total):
            at = pl.multiple_of(k * ROWS, ROWS)
            here = pl.ds(at, ROWS)
            inner = pl.ds(at + PAD, ROWS)
            held = {}

            def loaded(plane):
                if plane not in held:
                    held[plane] = three(field, plane, at)
                return held[plane]

            for x in which:
                picture, v = image(loaded, at, x)
                if iteration == 0:
                    residual = v - picture * inverse
                    direction = v * inverse
                else:
                    residual = res[x, here] - picture
                    direction = v
                if iteration < ITERS - 1:
                    res[x, here] = residual
                    a, b = factors[iteration]
                    fields[iteration + 1][x + 1, inner] = a * direction + b * residual
                else:
                    out_r[x, here] = residual
                    out_s[x, here] = v1[x + 1, inner] * inverse + v2[x + 1, inner] + v
                    total = total + residual * residual
            return total

        return lax.fori_loop(0, chunks, step, total)

    nothing = jnp.zeros(shape, jnp.float32)
    interior = range(1, planes - 1)
    edges = (0, planes - 1)

    load_lab.wait()
    lax.fori_loop(0, chunks, own_step, 0)
    coefficients(interior)
    load_rhs.wait()
    iterate(0, interior, 0)

    receive(0)
    for present, plane in ((has_left, 0), (has_right, planes + 1)):

        @pl.when(present)
        def _():
            def step(k, carry):
                look_up_x(plane, pl.multiple_of(k * ROWS, ROWS))
                return carry

            lax.fori_loop(0, chunks, step, 0)

    coefficients(edges)
    receive(1)
    iterate(0, edges, 0)
    send(2)
    iterate(1, interior, 0)
    receive(2)
    iterate(1, edges, 0)
    send(3)
    total = iterate(2, interior, nothing)

    def put(x):
        return [
            pltpu.make_async_copy(src.at[x], dst.at[x], out_sem.at[which, x])
            for which, (src, dst) in enumerate(((out_s, solution_hbm), (out_r, residual_hbm)))
        ]

    for x in interior:
        for copy in put(x):
            copy.start()
    receive(3)
    total = iterate(2, edges, total)
    for x in edges:
        for copy in put(x):
            copy.start()

    tile = jnp.zeros((8, LANES), jnp.float32)
    for r in range(ROWS // 8):
        for c in range(columns // LANES):
            tile = tile + total[r * 8 : (r + 1) * 8, c * LANES : (c + 1) * LANES]
    partial[...] = tile
    gathered[me] = tile

    def share(k):
        return pltpu.make_async_remote_copy(
            src_ref=partial,
            dst_ref=gathered.at[me],
            send_sem=psend.at[k],
            recv_sem=precv.at[me],
            device_id={"gz": lax.rem(me + k, n)},
            device_id_type=MESH,
        )

    def arrival(k):
        other = lax.rem(me + k, n)
        return pltpu.make_async_remote_copy(
            src_ref=partial,
            dst_ref=gathered.at[other],
            send_sem=psend.at[k],
            recv_sem=precv.at[other],
            device_id={"gz": other},
            device_id_type=MESH,
        )

    def start_share(k, carry):
        share(k).start()
        return carry

    def end_share(k, carry):
        arrival(k).wait_recv()
        return carry

    def end_send(k, carry):
        share(k).wait_send()
        return carry

    lax.fori_loop(1, n, start_share, 0)
    for kind in range(ITERS + 1):

        @pl.when(has_left)
        def _():
            to_left(kind).wait_send()

        @pl.when(has_right)
        def _():
            to_right(kind).wait_send()

    lax.fori_loop(1, n, end_share, 0)
    everything = lax.fori_loop(
        0, n, lambda k, t: t + gathered[k], jnp.zeros((8, LANES), jnp.float32)
    )
    squares = jnp.sum(everything)
    norm_ref[0] = jnp.sqrt(jnp.full((8, LANES), squares))[0, 0]
    lax.fori_loop(1, n, end_send, 0)
    for x in range(planes):
        for copy in put(x):
            copy.wait()


def per_device(labels, tensor_table, bounds, right_side):
    n = lax.axis_size("gz")
    planes, rows, columns = right_side.shape
    phases = tensor_table.shape[0]
    f32 = jnp.float32
    padded = rows + 2 * PAD

    def flat(count):
        return pltpu.VMEM((count, rows, columns), f32)

    def tall(count):
        return pltpu.VMEM((count, padded, columns), f32)

    any_spec = pl.BlockSpec(memory_space=pl.ANY)
    smem_spec = pl.BlockSpec(memory_space=pltpu.SMEM)
    return pl.pallas_call(
        functools.partial(kernel, n, planes, rows),
        out_shape=(
            jax.ShapeDtypeStruct(right_side.shape, f32),
            jax.ShapeDtypeStruct(right_side.shape, f32),
            jax.ShapeDtypeStruct((1,), f32),
        ),
        in_specs=[smem_spec, smem_spec, any_spec, any_spec],
        out_specs=(any_spec, any_spec, smem_spec),
        scratch_shapes=[
            pltpu.VMEM((planes + 2, rows, columns), jnp.int32),
            tall(planes + 2),
            tall(planes + 2),
            tall(planes + 2),
            flat(planes + 2),
            tall(planes + 2),
            flat(planes + 2),
            tall(planes),
            flat(planes),
            tall(planes),
            flat(planes),
            pltpu.VMEM((18, planes, rows, columns), f32),
            flat(planes),
            flat(planes),
            flat(planes),
            flat(planes),
            pltpu.SMEM((phases, 7), f32),
            pltpu.VMEM((8, LANES), f32),
            pltpu.VMEM((n, 8, LANES), f32),
            pltpu.SemaphoreType.DMA((2,)),
            pltpu.SemaphoreType.DMA((2, planes)),
            pltpu.SemaphoreType.DMA((ITERS + 1, 2)),
            pltpu.SemaphoreType.DMA((ITERS + 1, 2)),
            pltpu.SemaphoreType.DMA((n,)),
            pltpu.SemaphoreType.DMA((n,)),
        ],
        compiler_params=pltpu.CompilerParams(
            collective_id=0, has_side_effects=True, vmem_limit_bytes=60 * 1024 * 1024
        ),
    )(tensor_table, bounds, labels, right_side)


def solution(mesh):
    return jax.shard_map(
        per_device,
        mesh=mesh,
        in_specs=(
            P(("groups", "gz"), None, None),
            P("groups", None),
            P("groups"),
            P(("groups", "gz"), None, None),
        ),
        out_specs=(P(("groups", "gz"), None, None), P(("groups", "gz"), None, None), P("groups")),
        check_vma=False,
    )
```

time: 197 us -> 51 us (0.26)
  other arithmetic: 113 us -> 0 us
  Pallas kernels: 0 us -> 45 us
  blocking collectives: 34.3 us -> 0 us
  starting transfers between devices: 25.6 us -> 0 us
  local copies, waits for them, and re-layouts: 12.7 us -> 3.35 us
  waiting for transfers between devices: 4.89 us -> 0 us
  between operations: 5.93 us -> 2.39 us
    pallas_call x0 -> x1, Pallas kernels: none -> 45 us  [per_device(): pl.pallas_call(functools.partial(kernel, n, planes, rows), out_shape=(jax...]
    psum x1 -> x0, blocking collectives: 34.3 us -> none  [per_device(): squares = lax.psum(jnp.sum(residual * residual), 'gz')]
    add x3 -> x0, other arithmetic: 33.6 us -> none  [the longest x2 32.3 us: per_device(): new_factor * factor * direction + 2.0 * new_factor / spread * residual]
    select_n x4 -> x0, other arithmetic: 27.2 us -> none  [cell_values(): result = jnp.where(labels == phase, per_phase[phase], result)]
    unnamed x4 -> x0, other arithmetic: 27 us -> none
    ppermute x8 -> x0, starting transfers between devices: 25.6 us -> none  [the longest x4 20 us: extended_2(): lax.ppermute(tail, axis, [(i, (i + 1) % count) for i in range(ends)])]
    slice x11 -> x0, local copies, waits for them, and re-layouts: 10.2 us -> none  [the longest x4 4.85 us: extended_2(): lax.slice_in_dim(cells, cells.shape[dim] - width, cells.shape[dim], axis=...]
    reduce_sum x1 -> x0, other arithmetic: 10.1 us -> none  [per_device(): squares = lax.psum(jnp.sum(residual * residual), 'gz')]
  transfers between devices with their start and end apart: 8 -> 0, of which waited for: 2 -> 0; matrix products, arithmetic and copies ran while one was open for 36% -> 0% of each run, Pallas kernels for 0% -> 0%
where the time goes in v1:
time: 51 us; the launch traced here: 50.8 us
  Pallas kernels  45 us (88%)
  local copies, waits for them, and re-layouts  3.35 us (7%)
  between operations  2.39 us (5%)
    pallas_call x1, Pallas kernels, per_device(): pl.pallas_call(functools.partial(kernel, n, planes, rows), out_shape=(jax...  45 us
    unnamed x4, local copies, waits for them, and re-layouts  3.35 us

profile of v1, /device:TPU:0, one launch (start us, length us, event | category | flops | bytes accessed | tf_op | source)
XLA Modules:
  0.0 50.8 jit_solution(15026899306666324624)
XLA Ops:
  0.6 45.0 %shard_map.67 = (f32[4,256,256]{2,1,0:T(8,128)}, f32[4,256,256]{2,1,0:T(8,128)}, f32[1]{0:T(128)}) custom-call(f32[8,7]{1,0:T(8,128)} %table_ref.1, f32[2]{0:T(128)} %bounds_ref.1, s32[4,256,256]{2,1,0:T(8,128)} %labels_hbm.1, f32[4,256,256]{2,1,0:T(8,128)} %rhs_hbm.1), custom_call_target="tpu_custom_call" | custom-call | tf_op jit(solution)/shard_map/pallas_call | solution.py:433
  45.7 0.0 copy-start
  45.7 2.4 %copy.10 = f32[4,256,256]{2,1,0:T(8,128)} copy(f32[4,256,256]{2,1,0:T(8,128)} %get-tuple-element.6) | data formatting | bytes 2097152
  48.0 0.0 copy-done
  48.0 1.0 %copy.11 = f32[4,256,256]{2,1,0:T(8,128)} copy(f32[4,256,256]{2,1,0:T(8,128)S(1)} %copy-done) | data formatting | bytes 2097152
Async XLA Ops:
  45.7 2.4 %copy-start = (f32[4,256,256]{2,1,0:T(8,128)S(1)}, f32[4,256,256]{2,1,0:T(8,128)}, u32[]{:S(2)}) copy-start(f32[4,256,256]{2,1,0:T(8,128)} %get-tuple-element.7) | copy-start | bytes 3145732

commit v2 on v1

--- a/solution.py
+++ b/solution.py
@@ -11,6 +11,7 @@
 PAD = 8
 ROWS = 16
 LANES = 128
+PIECES = 4
 MESH = pl.DeviceIdType.MESH
 
 
@@ -48,6 +49,13 @@
     fields = (v1, v2, v3)
     chunks = rows // ROWS
     body_rows = pl.ds(PAD, rows)
+    piece = rows // PIECES
+
+    def span(kind, c):
+        lag = ROWS * max(kind - 1, 0)
+        low = piece * c - lag if c else 0
+        high = piece * (c + 1) - lag if c < PIECES - 1 else rows
+        return low, high
 
     barrier = pltpu.get_barrier_semaphore()
 
@@ -65,60 +73,60 @@
     load_lab = pltpu.make_async_copy(labels_hbm, lab.at[pl.ds(1, planes)], local_sem.at[1])
     load_lab.start()
     load_rhs.start()
-    pl.semaphore_wait(barrier, n - 1)
-
-    def views(kind, plane):
+
+    def views(kind, plane, c):
+        low, high = span(kind, c)
         if kind == 0:
-            return lab.at[plane]
-        return fields[kind - 1].at[plane, body_rows]
-
-    def source(kind, plane):
+            return lab.at[plane, pl.ds(low, high - low)]
+        return fields[kind - 1].at[plane, pl.ds(low + PAD, high - low)]
+
+    def source(kind, plane, c):
+        low, high = span(kind, c)
         if kind == 0:
-            return labels_hbm.at[plane]
+            return labels_hbm.at[plane, pl.ds(low, high - low)]
         if kind == 1:
-            return rhs_hbm.at[plane]
-        return fields[kind - 1].at[plane + 1, body_rows]
-
-    def to_left(kind):
+            return rhs_hbm.at[plane, pl.ds(low, high - low)]
+        return fields[kind - 1].at[plane + 1, pl.ds(low + PAD, high - low)]
+
+    def to_left(kind, c):
         return pltpu.make_async_remote_copy(
-            src_ref=source(kind, 0),
-            dst_ref=views(kind, planes + 1),
-            send_sem=send_sem.at[kind, 0],
-            recv_sem=recv_sem.at[kind, 0],
+            src_ref=source(kind, 0, c),
+            dst_ref=views(kind, planes + 1, c),
+            send_sem=send_sem.at[kind, c, 0],
+            recv_sem=recv_sem.at[kind, c, 0],
             device_id={"gz": left},
             device_id_type=MESH,
         )
 
-    def to_right(kind):
+    def to_right(kind, c):
         return pltpu.make_async_remote_copy(
-            src_ref=source(kind, planes - 1),
-            dst_ref=views(kind, 0),
-            send_sem=send_sem.at[kind, 1],
-            recv_sem=recv_sem.at[kind, 1],
+            src_ref=source(kind, planes - 1, c),
+            dst_ref=views(kind, 0, c),
+            send_sem=send_sem.at[kind, c, 1],
+            recv_sem=recv_sem.at[kind, c, 1],
             device_id={"gz": right},
             device_id_type=MESH,
         )
 
-    def send(kind):
+    def send(*kinds_at):
         @pl.when(has_left)
         def _():
-            to_left(kind).start()
+            for kind, c in kinds_at:
+                to_left(kind, c).start()
 
         @pl.when(has_right)
         def _():
-            to_right(kind).start()
-
-    def receive(kind):
+            for kind, c in kinds_at:
+                to_right(kind, c).start()
+
+    def receive(kind, c):
         @pl.when(has_left)
         def _():
-            to_right(kind).wait_recv()
+            to_right(kind, c).wait_recv()
 
         @pl.when(has_right)
         def _():
-            to_left(kind).wait_recv()
-
-    send(0)
-    send(1)
+            to_left(kind, c).wait_recv()
 
     for phase in range(weight.shape[0]):
         k_xx, k_yy, k_zz, k_xy, k_xz, k_yz, m = [table_ref[phase, c] for c in range(7)]
@@ -157,6 +165,10 @@
     @pl.when(me == n - 1)
     def _():
         clear(planes + 1)
+
+    pl.semaphore_wait(barrier, n - 1)
+    for c in range(PIECES):
+        send((0, c), (1, c))
 
     def look_up(plane, at, which):
         label = lab[plane, pl.ds(at, ROWS)]
@@ -202,7 +214,7 @@
             pltpu.roll(wide, 1, 0)[PAD : PAD + ROWS],
         )
 
-    def coefficients(which):
+    def coefficients(which, low, high):
         def step(k, carry):
             at = pl.multiple_of(k * ROWS, ROWS)
             here = pl.ds(at, ROWS)
@@ -239,7 +251,7 @@
                 diag[x, here] = total
             return carry
 
-        lax.fori_loop(0, chunks, step, 0)
+        lax.fori_loop(low // ROWS, high // ROWS, step, 0)
 
     def image(loaded, at, x):
         here = pl.ds(at, ROWS)
@@ -272,7 +284,7 @@
         factors.append((new_factor * factor, 2.0 * new_factor / spread))
         factor = new_factor
 
-    def iterate(iteration, which, total):
+    def iterate(iteration, which, total, low, high):
         field = fields[iteration]
 
         def step(k, total):
@@ -304,7 +316,7 @@
                     total = total + residual * residual
             return total
 
-        return lax.fori_loop(0, chunks, step, total)
+        return lax.fori_loop(low // ROWS, high // ROWS, step, total)
 
     nothing = jnp.zeros(shape, jnp.float32)
     interior = range(1, planes - 1)
@@ -312,30 +324,33 @@
 
     load_lab.wait()
     lax.fori_loop(0, chunks, own_step, 0)
-    coefficients(interior)
+    coefficients(interior, 0, rows)
     load_rhs.wait()
-    iterate(0, interior, 0)
-
-    receive(0)
-    for present, plane in ((has_left, 0), (has_right, planes + 1)):
-
-        @pl.when(present)
-        def _():
-            def step(k, carry):
-                look_up_x(plane, pl.multiple_of(k * ROWS, ROWS))
-                return carry
-
-            lax.fori_loop(0, chunks, step, 0)
-
-    coefficients(edges)
-    receive(1)
-    iterate(0, edges, 0)
-    send(2)
-    iterate(1, interior, 0)
-    receive(2)
-    iterate(1, edges, 0)
-    send(3)
-    total = iterate(2, interior, nothing)
+    iterate(0, interior, 0, 0, rows)
+
+    for c in range(PIECES):
+        receive(0, c)
+        low, high = span(0, c)
+        for present, plane in ((has_left, 0), (has_right, planes + 1)):
+
+            @pl.when(present)
+            def _():
+                def step(k, carry):
+                    look_up_x(plane, pl.multiple_of(k * ROWS, ROWS))
+                    return carry
+
+                lax.fori_loop(low // ROWS, high // ROWS, step, 0)
+
+        coefficients(edges, *span(2, c))
+        receive(1, c)
+        iterate(0, edges, 0, *span(2, c))
+        send((2, c))
+    iterate(1, interior, 0, 0, rows)
+    for c in range(PIECES):
+        receive(2, c)
+        iterate(1, edges, 0, *span(3, c))
+        send((3, c))
+    total = iterate(2, interior, nothing, 0, rows)
 
     def put(x):
         return [
@@ -346,8 +361,9 @@
     for x in interior:
         for copy in put(x):
             copy.start()
-    receive(3)
-    total = iterate(2, edges, total)
+    for c in range(PIECES):
+        receive(3, c)
+        total = iterate(2, edges, total, *span(4, c))
     for x in edges:
         for copy in put(x):
             copy.start()
@@ -393,15 +409,18 @@
         return carry
 
     lax.fori_loop(1, n, start_share, 0)
-    for kind in range(ITERS + 1):
-
-        @pl.when(has_left)
-        def _():
-            to_left(kind).wait_send()
-
-        @pl.when(has_right)
-        def _():
-            to_right(kind).wait_send()
+
+    @pl.when(has_left)
+    def _():
+        for kind in range(ITERS + 1):
+            for c in range(PIECES):
+                to_left(kind, c).wait_send()
+
+    @pl.when(has_right)
+    def _():
+        for kind in range(ITERS + 1):
+            for c in range(PIECES):
+                to_right(kind, c).wait_send()
 
     lax.fori_loop(1, n, end_share, 0)
     everything = lax.fori_loop(
@@ -461,8 +480,8 @@
             pltpu.VMEM((n, 8, LANES), f32),
             pltpu.SemaphoreType.DMA((2,)),
             pltpu.SemaphoreType.DMA((2, planes)),
-            pltpu.SemaphoreType.DMA((ITERS + 1, 2)),
-            pltpu.SemaphoreType.DMA((ITERS + 1, 2)),
+            pltpu.SemaphoreType.DMA((ITERS + 1, PIECES, 2)),
+            pltpu.SemaphoreType.DMA((ITERS + 1, PIECES, 2)),
             pltpu.SemaphoreType.DMA((n,)),
             pltpu.SemaphoreType.DMA((n,)),
         ],

time: 51 us -> 43.4 us (0.85)
  Pallas kernels: 45 us -> 37.4 us
    pallas_call x1, Pallas kernels: 45 us -> 37.4 us  [per_device(): pl.pallas_call(functools.partial(kernel, n, planes, rows), out_shape=(jax...]
where the time goes in v2:
time: 43.4 us; the launch traced here: 43.1 us
  Pallas kernels  37.4 us (86%)
  local copies, waits for them, and re-layouts  3.35 us (8%)
  between operations  2.39 us (6%)
    pallas_call x1, Pallas kernels, per_device(): pl.pallas_call(functools.partial(kernel, n, planes, rows), out_shape=(jax...  37.4 us
    unnamed x4, local copies, waits for them, and re-layouts  3.35 us

profile of v2, /device:TPU:0, one launch (start us, length us, event | category | flops | bytes accessed | tf_op | source)
XLA Modules:
  0.0 43.1 jit_solution(14804716703910312678)
XLA Ops:
  0.6 37.4 %shard_map.67 = (f32[4,256,256]{2,1,0:T(8,128)}, f32[4,256,256]{2,1,0:T(8,128)}, f32[1]{0:T(128)}) custom-call(f32[8,7]{1,0:T(8,128)} %table_ref.1, f32[2]{0:T(128)} %bounds_ref.1, s32[4,256,256]{2,1,0:T(8,128)} %labels_hbm.1, f32[4,256,256]{2,1,0:T(8,128)} %rhs_hbm.1), custom_call_target="tpu_custom_call" | custom-call | tf_op jit(solution)/shard_map/pallas_call | solution.py:452
  38.0 0.0 copy-start
  38.1 2.4 %copy.10 = f32[4,256,256]{2,1,0:T(8,128)} copy(f32[4,256,256]{2,1,0:T(8,128)} %get-tuple-element.6) | data formatting | bytes 2097152
  40.4 0.0 copy-done
  40.4 1.0 %copy.11 = f32[4,256,256]{2,1,0:T(8,128)} copy(f32[4,256,256]{2,1,0:T(8,128)S(1)} %copy-done) | data formatting | bytes 2097152
Async XLA Ops:
  38.0 2.4 %copy-start = (f32[4,256,256]{2,1,0:T(8,128)S(1)}, f32[4,256,256]{2,1,0:T(8,128)}, u32[]{:S(2)}) copy-start(f32[4,256,256]{2,1,0:T(8,128)} %get-tuple-element.7) | copy-start | bytes 3145732

commit v3 on v2

--- a/solution.py
+++ b/solution.py
@@ -38,10 +38,10 @@
 
 
 def kernel(
-    n, planes, rows, table_ref, bounds_ref, labels_hbm, rhs_hbm,
-    solution_hbm, residual_hbm, norm_ref,
-    lab, v1, v2, v3, hx, kxy, kxz, hy, hz, kyz, react, coef, diag, res, out_s, out_r,
-    weight, partial, gathered, local_sem, out_sem, send_sem, recv_sem, psend, precv,
+    n, planes, rows, table_hbm, bounds_hbm, labels_hbm, rhs_hbm,
+    out_s, out_r, norm_ref,
+    lab, v1, v2, v3, hx, kxy, kxz, hy, hz, kyz, react, coef, diag, res,
+    table_ref, bounds_ref, weight, partial, gathered, known, local_sem, send_sem, recv_sem, psend, precv,
 ):
     me = lax.axis_index("gz")
     left, right = me - 1, me + 1
@@ -59,18 +59,44 @@
 
     barrier = pltpu.get_barrier_semaphore()
 
-    def greet(k, carry):
-        pl.semaphore_signal(
-            barrier, inc=1, device_id={"gz": lax.rem(me + k, n)}, device_id_type=MESH
-        )
-        return carry
-
-    lax.fori_loop(1, n, greet, 0)
+    @pl.when(has_left)
+    def _():
+        pl.semaphore_signal(barrier, inc=1, device_id={"gz": left}, device_id_type=MESH)
+
+    @pl.when(has_right)
+    def _():
+        pl.semaphore_signal(barrier, inc=1, device_id={"gz": right}, device_id_type=MESH)
+
+    distances = []
+    while 2 * 2 ** len(distances) < n - 1:
+        distances.append(2 * 2 ** len(distances))
+
+    def within(distance):
+        below = jnp.where(me - distance >= 0, 1, 0)
+        above = jnp.where(me + distance < n, 1, 0)
+        return below + above
+
+    def call(round_):
+        distance = distances[round_]
+        for other in (me - distance, me + distance):
+
+            @pl.when((other >= 0) & (other < n))
+            def _():
+                pl.semaphore_signal(
+                    known.at[round_], inc=1, device_id={"gz": other}, device_id_type=MESH
+                )
+
+    def heed(round_):
+        pl.semaphore_wait(known.at[round_], within(distances[round_]))
 
     load_rhs = pltpu.make_async_copy(
         rhs_hbm, v1.at[pl.ds(1, planes), body_rows], local_sem.at[0]
     )
     load_lab = pltpu.make_async_copy(labels_hbm, lab.at[pl.ds(1, planes)], local_sem.at[1])
+    load_table = pltpu.make_async_copy(table_hbm, table_ref, local_sem.at[2])
+    load_bounds = pltpu.make_async_copy(bounds_hbm, bounds_ref, local_sem.at[3])
+    load_table.start()
+    load_bounds.start()
     load_lab.start()
     load_rhs.start()
 
@@ -128,6 +154,40 @@
         def _():
             to_left(kind, c).wait_recv()
 
+    columns = v1.shape[2]
+    strip = jnp.zeros((PAD, columns), jnp.float32)
+    for ref in (v1, v2, v3, kxy, hy, kyz):
+        for plane in range(ref.shape[0]):
+            ref[plane, pl.ds(0, PAD)] = strip
+            ref[plane, pl.ds(PAD + rows, PAD)] = strip
+
+    def clear(plane):
+        zero = jnp.zeros((ROWS, columns), jnp.float32)
+
+        def step(k, carry):
+            at = pl.multiple_of(k * ROWS, ROWS)
+            for ref in (v1, v2, v3, kxy):
+                ref[plane, pl.ds(at + PAD, ROWS)] = zero
+            for ref in (hx, kxz):
+                ref[plane, pl.ds(at, ROWS)] = zero
+            return carry
+
+        lax.fori_loop(0, chunks, step, 0)
+
+    @pl.when(me == 0)
+    def _():
+        clear(0)
+
+    @pl.when(me == n - 1)
+    def _():
+        clear(planes + 1)
+
+    pl.semaphore_wait(barrier, within(1))
+    for c in range(PIECES):
+        send((0, c), (1, c))
+
+    load_table.wait()
+    load_bounds.wait()
     for phase in range(weight.shape[0]):
         k_xx, k_yy, k_zz, k_xy, k_xz, k_yz, m = [table_ref[phase, c] for c in range(7)]
         weight[phase, 0] = 0.5 * (k_xx - jnp.abs(k_xy) - jnp.abs(k_xz))
@@ -137,38 +197,6 @@
         weight[phase, 4] = 0.5 * k_xz
         weight[phase, 5] = 0.5 * k_yz
         weight[phase, 6] = m
-
-    columns = v1.shape[2]
-    strip = jnp.zeros((PAD, columns), jnp.float32)
-    for ref in (v1, v2, v3, kxy, hy, kyz):
-        for plane in range(ref.shape[0]):
-            ref[plane, pl.ds(0, PAD)] = strip
-            ref[plane, pl.ds(PAD + rows, PAD)] = strip
-
-    def clear(plane):
-        zero = jnp.zeros((ROWS, columns), jnp.float32)
-
-        def step(k, carry):
-            at = pl.multiple_of(k * ROWS, ROWS)
-            for ref in (v1, v2, v3, kxy):
-                ref[plane, pl.ds(at + PAD, ROWS)] = zero
-            for ref in (hx, kxz):
-                ref[plane, pl.ds(at, ROWS)] = zero
-            return carry
-
-        lax.fori_loop(0, chunks, step, 0)
-
-    @pl.when(me == 0)
-    def _():
-        clear(0)
-
-    @pl.when(me == n - 1)
-    def _():
-        clear(planes + 1)
-
-    pl.semaphore_wait(barrier, n - 1)
-    for c in range(PIECES):
-        send((0, c), (1, c))
 
     def look_up(plane, at, which):
         label = lab[plane, pl.ds(at, ROWS)]
@@ -345,28 +373,24 @@
         receive(1, c)
         iterate(0, edges, 0, *span(2, c))
         send((2, c))
+        if c == 0 and distances:
+            call(0)
     iterate(1, interior, 0, 0, rows)
     for c in range(PIECES):
         receive(2, c)
         iterate(1, edges, 0, *span(3, c))
         send((3, c))
+        if c < len(distances) - 1:
+            heed(c)
+            call(c + 1)
+    for round_ in range(PIECES, len(distances) - 1):
+        heed(round_)
+        call(round_ + 1)
     total = iterate(2, interior, nothing, 0, rows)
 
-    def put(x):
-        return [
-            pltpu.make_async_copy(src.at[x], dst.at[x], out_sem.at[which, x])
-            for which, (src, dst) in enumerate(((out_s, solution_hbm), (out_r, residual_hbm)))
-        ]
-
-    for x in interior:
-        for copy in put(x):
-            copy.start()
     for c in range(PIECES):
         receive(3, c)
         total = iterate(2, edges, total, *span(4, c))
-    for x in edges:
-        for copy in put(x):
-            copy.start()
 
     tile = jnp.zeros((8, LANES), jnp.float32)
     for r in range(ROWS // 8):
@@ -408,6 +432,8 @@
         share(k).wait_send()
         return carry
 
+    if distances:
+        heed(len(distances) - 1)
     lax.fori_loop(1, n, start_share, 0)
 
     @pl.when(has_left)
@@ -429,9 +455,6 @@
     squares = jnp.sum(everything)
     norm_ref[0] = jnp.sqrt(jnp.full((8, LANES), squares))[0, 0]
     lax.fori_loop(1, n, end_send, 0)
-    for x in range(planes):
-        for copy in put(x):
-            copy.wait()
 
 
 def per_device(labels, tensor_table, bounds, right_side):
@@ -448,6 +471,7 @@
         return pltpu.VMEM((count, padded, columns), f32)
 
     any_spec = pl.BlockSpec(memory_space=pl.ANY)
+    vmem_spec = pl.BlockSpec(memory_space=pltpu.VMEM)
     smem_spec = pl.BlockSpec(memory_space=pltpu.SMEM)
     return pl.pallas_call(
         functools.partial(kernel, n, planes, rows),
@@ -456,8 +480,8 @@
             jax.ShapeDtypeStruct(right_side.shape, f32),
             jax.ShapeDtypeStruct((1,), f32),
         ),
-        in_specs=[smem_spec, smem_spec, any_spec, any_spec],
-        out_specs=(any_spec, any_spec, smem_spec),
+        in_specs=[any_spec] * 4,
+        out_specs=(vmem_spec, vmem_spec, smem_spec),
         scratch_shapes=[
             pltpu.VMEM((planes + 2, rows, columns), jnp.int32),
             tall(planes + 2),
@@ -473,22 +497,27 @@
             pltpu.VMEM((18, planes, rows, columns), f32),
             flat(planes),
             flat(planes),
-            flat(planes),
-            flat(planes),
+            pltpu.SMEM((phases, 7), f32),
+            pltpu.SMEM((2,), f32),
             pltpu.SMEM((phases, 7), f32),
             pltpu.VMEM((8, LANES), f32),
             pltpu.VMEM((n, 8, LANES), f32),
-            pltpu.SemaphoreType.DMA((2,)),
-            pltpu.SemaphoreType.DMA((2, planes)),
+            pltpu.SemaphoreType.REGULAR((max(n.bit_length(), 1),)),
+            pltpu.SemaphoreType.DMA((4,)),
             pltpu.SemaphoreType.DMA((ITERS + 1, PIECES, 2)),
             pltpu.SemaphoreType.DMA((ITERS + 1, PIECES, 2)),
             pltpu.SemaphoreType.DMA((n,)),
             pltpu.SemaphoreType.DMA((n,)),
         ],
         compiler_params=pltpu.CompilerParams(
-            collective_id=0, has_side_effects=True, vmem_limit_bytes=60 * 1024 * 1024
+            collective_id=0, has_side_effects=True, vmem_limit_bytes=44 * 1024 * 1024
         ),
-    )(tensor_table, bounds, labels, right_side)
+    )(
+        *[
+            pltpu.with_memory_space_constraint(array, pltpu.HBM)
+            for array in (tensor_table, bounds, labels, right_side)
+        ]
+    )
 
 
 def solution(mesh):

time: 43.4 us -> 40.2 us (0.926)
  Pallas kernels: 37.4 us -> 35.8 us
  local copies, waits for them, and re-layouts: 3.35 us -> 1.94 us
    pallas_call x1, Pallas kernels: 37.4 us -> 35.8 us  [per_device(): pl.pallas_call(functools.partial(kernel, n, planes, rows), out_shape=(jax...]
    unnamed x4 -> x2, local copies, waits for them, and re-layouts: 3.35 us -> 1.94 us
where the time goes in v3:
time: 40.2 us; the launch traced here: 40 us
  Pallas kernels  35.8 us (89%)
  between operations  2.33 us (6%)
  local copies, waits for them, and re-layouts  1.94 us (5%)
    pallas_call x1, Pallas kernels, per_device(): pl.pallas_call(functools.partial(kernel, n, planes, rows), out_shape=(jax...  35.8 us
    unnamed x2, local copies, waits for them, and re-layouts  1.94 us

profile of v3, /device:TPU:0, one launch (start us, length us, event | category | flops | bytes accessed | tf_op | source)
XLA Modules:
  0.0 40.0 jit_solution(529799711023857638)
XLA Ops:
  0.6 35.8 %shard_map.67 = (f32[4,256,256]{2,1,0:T(8,128)S(1)}, f32[4,256,256]{2,1,0:T(8,128)S(1)}, f32[1]{0:T(128)}) custom-call(f32[8,7]{1,0:T(8,128)} %table_hbm.1, f32[2]{0:T(128)} %bounds_hbm.1, s32[4,256,256]{2,1,0:T(8,128)} %labels_hbm.1, f32[4,256,256]{2,1,0:T(8,128)} %rhs_hbm.1), custom_call_target="tpu_custom_call" | custom-call | tf_op jit(solution)/shard_map/pallas_call | solution.py:476
  36.4 1.0 %copy.10 = f32[4,256,256]{2,1,0:T(8,128)} copy(f32[4,256,256]{2,1,0:T(8,128)S(1)} %get-tuple-element.6) | data formatting | bytes 2097152
  37.4 1.0 %copy.11 = f32[4,256,256]{2,1,0:T(8,128)} copy(f32[4,256,256]{2,1,0:T(8,128)S(1)} %get-tuple-element.7) | data formatting | bytes 2097152
